TPU v7x, 32 devices: a whole 2x2x4 slice. The times are simulated.
32 devices in a mesh: row: 8 (over z, x), col: 4 (over y, core).
Axes of the slice: x: 2, y: 2, z: 4, core: 2. Of those that a mesh axis runs over, the one named last changes fastest.
Arguments:
- coeffs: float32 [4096, 4096], P('row', 'col'), may hold values from -6 to 6
- ham_alpha: float32 [4096, 4096], P('row'), may hold values from -1.5 to 7.5, as said below
- ham_beta: float32 [4096, 4096], P('col'), may hold values from -1.5 to 7.5, as said below
Outputs:
- sigma_vec: float32 [4096, 4096], P('row', 'col')
Inputs may be any that keep to these rules, and one draw needn't show every extreme that they name: `ham_alpha`: symmetric. `ham_beta`: symmetric.
All inputs are finite; a program needn't handle non-finite values.
Results may differ from a plain program's by a relative error of at most 0.00005.
Values sent between devices are 32-bit elements; how exact they have to be, the bound alone decides.
A program may use at most 128 MiB of HBM per device.

v0:
```python
import jax
import jax.numpy as jnp
from jax import lax
from jax.sharding import PartitionSpec as P

HIGHEST = lax.Precision.HIGHEST


def local(coeffs, ham_alpha, ham_beta):
    ham_cols = ham_alpha
    alpha_part = jnp.dot(
        ham_cols,
        lax.all_gather(coeffs, "row", axis=0, tiled=True),
        precision=HIGHEST,
        preferred_element_type=jnp.float32,
    )
    ham_cols = ham_beta
    flipped = lax.psum_scatter(
        lax.dot_general(
            ham_cols,
            coeffs,
            (((0,), (1,)), ((), ())),
            precision=HIGHEST,
            preferred_element_type=jnp.float32,
        ),
        "col",
        scatter_dimension=0,
        tiled=True,
    )
    beta_part = flipped.T
    return alpha_part + beta_part


def solution(mesh):
    in_specs = (P("row", "col"), P("row", None), P("col", None))
    out_specs = P("row", "col")
    return jax.shard_map(local, mesh=mesh, in_specs=in_specs, out_specs=out_specs, check_vma=False)
```

profile of v0, /device:TPU:0, one launch (start us, length us, event | category | flops | bytes accessed | tf_op | source)
XLA Modules:
  0.0 311.4 jit_solution(360071280778495948)
XLA Ops:
  7.4 0.0 reduce-scatter.2.cloned.1.call-start
  7.4 31.3 %fusion = f32[4096,512]{0,1:T(8,128)} fusion(f32[1024,4096]{1,0:T(8,128)} %param.5, f32[512,1024]{1,0:T(8,128)} %param.3), kind=kOutput, calls=%fused_computation.1 | convolution fusion | flops 25769803776 | bytes 27262976 | tf_op jit(solution)/shard_map/dot_general | solution.py:19
  38.7 0.0 reduce-scatter.2.cloned.1.call-update
  38.7 0.2 all-gather.2.cloned.1.call-start
  39.0 0.3 all-gather.2.cloned.1.call-update
  39.3 73.5 %reduce-scatter.2.cloned.1.call-done = f32[1024,512]{0,1:T(8,128)} async-done(((f32[4096,512]{0,1:T(8,128)}), f32[1024,512]{0,1:T(8,128)}) %reduce-scatter.2.cloned.1.call-update) | async-done | bytes 2097168 | tf_op jit(solution)/shard_map/reduce_scatter | solution.py:18
  112.8 158.3 %all-gather.2.cloned.1.call-done = f32[4096,1024]{1,0:T(8,128)} async-done(((f32[512,1024]{1,0:T(8,128)}), f32[4096,1024]{1,0:T(8,128)}) %all-gather.2.cloned.1.call-update) | async-done | bytes 16777232 | tf_op jit(solution)/shard_map/all_gather | solution.py:13
  271.2 32.7 %bitcast_add_fusion = f32[512,1024]{1,0:T(8,128)} fusion(f32[1024,512]{0,1:T(8,128)} %reduce-scatter.2.cloned.1.call-done, f32[512,4096]{1,0:T(8,128)} %param.4, f32[4096,1024]{1,0:T(8,128)} %all-gather.2.cloned.1.call-done), kind=kOutput, calls=%fused_computation | convolution fusion | flops 25770328064 | bytes 29360128 | tf_op jit(solution)/shard_map/dot_general | solution.py:11
Async XLA Ops:
  7.4 105.5 %reduce-scatter.2.cloned.1.call-start = ((), (), s32[]{:S(2)}) async-start(), calls=%async_computation.2 | async-start | bytes 10485760 | tf_op jit(solution)/shard_map/reduce_scatter | solution.py:18
  38.7 232.5 %all-gather.2.cloned.1.call-start = ((), (), s32[]{:S(2)}) async-start(), calls=%async_computation.1 | async-start | bytes 18874368 | tf_op jit(solution)/shard_map/all_gather | solution.py:13
Sparse Core Ops, SparseCore 0:
  38.8 73.9 reduce-scatter.1
Sparse Core Ops, SparseCore 1:
  41.3 229.8 all-gather.1
where the time goes:
time: 312 us; the launch traced here: 311 us
  waiting for transfers between devices  232 us (74%)
  matrix products  64.1 us (21%)
  between operations  14.8 us (5%)
    all_gather x1, waiting for transfers between devices, local(): lax.all_gather(coeffs, 'row', axis=0, tiled=True)  158 us
    reduce_scatter x1, waiting for transfers between devices, local(): lax.psum_scatter(lax.dot_general(ham_cols, coeffs, (((0,), (1,)), ((), ()...  73.5 us
    dot_general x1, matrix products, local(): jnp.dot(ham_cols, lax.all_gather(coeffs, 'row', axis=0, tiled=True), prec...  32.7 us
    dot_general x1, matrix products, local(): lax.dot_general(ham_cols, coeffs, (((0,), (1,)), ((), ())), precision=HIG...  31.3 us
  transfers between devices with their start and end apart: 2, of which 2 were waited for; matrix products, arithmetic and copies ran while one was open for 0% of the time, Pallas kernels for 0%

commit v1 on v0

--- a/solution.py
+++ b/solution.py
@@ -6,13 +6,20 @@
 HIGHEST = lax.Precision.HIGHEST
 
 
+def collect(x, axis, dim):
+    ways, here, step = (lax.axis_size(axis), lax.axis_index(axis), x.shape[dim])
+    shape = [n * ways if d == dim else n for d, n in enumerate(x.shape)]
+    full = lax.dynamic_update_slice_in_dim(jnp.zeros(shape, x.dtype), x, here * step, axis=dim)
+    for far in range(1, ways):
+        x = lax.ppermute(x, axis, [(d, (d + 1) % ways) for d in range(ways)])
+        full = lax.dynamic_update_slice_in_dim(full, x, (here - far) % ways * step, axis=dim)
+    return full
+
+
 def local(coeffs, ham_alpha, ham_beta):
     ham_cols = ham_alpha
     alpha_part = jnp.dot(
-        ham_cols,
-        lax.all_gather(coeffs, "row", axis=0, tiled=True),
-        precision=HIGHEST,
-        preferred_element_type=jnp.float32,
+        ham_cols, collect(coeffs, "row", 0), precision=HIGHEST, preferred_element_type=jnp.float32
     )
     ham_cols = ham_beta
     flipped = lax.psum_scatter(

time: 312 us -> 475 us (1.52)
  waiting for transfers between devices: 232 us -> 312 us
  matrix products: 64.1 us -> 114 us
  local copies, waits for them, and re-layouts: 0 us -> 32.6 us
    ppermute x0 -> x7, waiting for transfers between devices: none -> 312 us  [collect(): x = lax.ppermute(x, axis, [(d, (d + 1) % ways) for d in range(ways)])]
    all_gather x1 -> x0, waiting for transfers between devices: 158 us -> none  [local(): lax.all_gather(coeffs, 'row', axis=0, tiled=True)]
    reduce_scatter x1, waiting for transfers between devices: 73.5 us -> 0.01 us  [local(): lax.psum_scatter(lax.dot_general(ham_cols, coeffs, (((0,), (1,)), ((), ()...]
    dot_general x1, matrix products: 31.3 us -> 57.6 us  [local(): lax.dot_general(ham_cols, coeffs, (((0,), (1,)), ((), ())), precision=HIG...]
    dot_general x1, matrix products: 32.7 us -> 56.3 us  [local(): jnp.dot(ham_cols, collect(coeffs, 'row', 0), precision=HIGHEST, preferred...]
    dynamic_update_slice x0 -> x8, local copies, waits for them, and re-layouts: none -> 15.3 us  [the longest x7 13.8 us: collect(): lax.dynamic_update_slice_in_dim(full, x, (here - far) % ways * step, axis...]
    broadcast_in_dim x0 -> x1, local copies, waits for them, and re-layouts: none -> 8.74 us  [collect(): jnp.zeros(shape, x.dtype)]
    unnamed x0 -> x22, local copies, waits for them, and re-layouts: none -> 6.67 us
  transfers between devices with their start and end apart: 2 -> 8, of which waited for: 2 -> 7; matrix products, arithmetic and copies ran while one was open for 0% -> 5% of each run, Pallas kernels for 0% -> 0%
where the time goes in v1:
time: 475 us
  waiting for transfers between devices  312 us (66%)
  matrix products  114 us (24%)
  local copies, waits for them, and re-layouts  32.6 us (7%)
  between operations  13.4 us (3%)
    ppermute x7, waiting for transfers between devices, collect(): x = lax.ppermute(x, axis, [(d, (d + 1) % ways) for d in range(ways)])  312 us
    dot_general x1, matrix products, local(): lax.dot_general(ham_cols, coeffs, (((0,), (1,)), ((), ())), precision=HIG...  57.6 us
    dot_general x1, matrix products, local(): jnp.dot(ham_cols, collect(coeffs, 'row', 0), precision=HIGHEST, preferred...  56.3 us
    dynamic_update_slice x7, local copies, waits for them, and re-layouts, collect(): lax.dynamic_update_slice_in_dim(full, x, (here - far) % ways * step, axis...  13.8 us
  transfers between devices with their start and end apart: 8, of which 7 were waited for; matrix products, arithmetic and copies ran while one was open for 5% of the time, Pallas kernels for 0%

profile of v1, /device:TPU:0, one launch (start us, length us, event | category | flops | bytes accessed | tf_op | source)
XLA Modules:
  0.0 475.2 jit_solution(5197545258428441978)
XLA Ops:
  6.5 0.0 copy-start
  6.5 0.0 reduce-scatter.2.cloned.1.call-start
  6.5 57.6 %fusion = f32[4096,512]{1,0:T(8,128)} fusion(f32[1024,4096]{1,0:T(8,128)} %param.5, f32[512,1024]{1,0:T(8,128)} %param.3), kind=kOutput, calls=%fused_computation.9 | convolution fusion | flops 25769803776 | bytes 27262976 | tf_op jit(solution)/shard_map/dot_general | solution.py:26
  64.2 0.0 reduce-scatter.2.cloned.1.call-update
  64.2 0.0 copy-done
  64.2 3.0 collective-permute-start
  67.2 48.7 %collective-permute-done = f32[512,1024]{1,0:T(8,128)S(1)} collective-permute-done((f32[512,1024]{1,0:T(8,128)S(1)}, f32[512,1024]{1,0:T(8,128)S(1)}, u32[]{:S(2)}, u32[]{:S(2)}) %collective-permute-start) | collective-permute-done | bytes 2097184 | tf_op jit(solution)/shard_map/ppermute | solution.py:14
  115.9 0.0 copy-start.1
  115.9 1.3 copy-done.1
  117.2 0.0 collective-permute-start.1
  117.2 49.5 %collective-permute-done.1 = f32[512,1024]{1,0:T(8,128)S(1)} collective-permute-done((f32[512,1024]{1,0:T(8,128)S(1)}, f32[512,1024]{1,0:T(8,128)S(1)}, u32[]{:S(2)}, u32[]{:S(2)}) %collective-permute-start.1) | collective-permute-done | bytes 2097184 | tf_op jit(solution)/shard_map/ppermute | solution.py:14
  166.7 0.0 copy-start.3
  166.7 1.3 copy-done.3
  168.0 0.0 collective-permute-start.2
  168.0 48.6 %collective-permute-done.2 = f32[512,1024]{1,0:T(8,128)S(1)} collective-permute-done((f32[512,1024]{1,0:T(8,128)S(1)}, f32[512,1024]{1,0:T(8,128)S(1)}, u32[]{:S(2)}, u32[]{:S(2)}) %collective-permute-start.2) | collective-permute-done | bytes 2097184 | tf_op jit(solution)/shard_map/ppermute | solution.py:14
  216.6 1.4 copy-done.5
  218.0 0.0 collective-permute-start.3
  218.1 47.8 %collective-permute-done.3 = f32[512,1024]{1,0:T(8,128)S(1)} collective-permute-done((f32[512,1024]{1,0:T(8,128)S(1)}, f32[512,1024]{1,0:T(8,128)S(1)}, u32[]{:S(2)}, u32[]{:S(2)}) %collective-permute-start.3) | collective-permute-done | bytes 2097184 | tf_op jit(solution)/shard_map/ppermute | solution.py:14
  265.8 0.0 copy-start.7
  265.8 1.3 copy-done.7
  267.1 0.0 collective-permute-start.4
  267.1 46.9 %collective-permute-done.4 = f32[512,1024]{1,0:T(8,128)S(1)} collective-permute-done((f32[512,1024]{1,0:T(8,128)S(1)}, f32[512,1024]{1,0:T(8,128)S(1)}, u32[]{:S(2)}, u32[]{:S(2)}) %collective-permute-start.4) | collective-permute-done | bytes 2097184 | tf_op jit(solution)/shard_map/ppermute | solution.py:14
  314.1 0.0 copy-start.9
  314.1 1.3 copy-done.9
  315.4 0.0 collective-permute-start.5
  315.4 46.2 %collective-permute-done.5 = f32[512,1024]{1,0:T(8,128)} collective-permute-done((f32[512,1024]{1,0:T(8,128)S(1)}, f32[512,1024]{1,0:T(8,128)}, u32[]{:S(2)}, u32[]{:S(2)}) %collective-permute-start.5) | collective-permute-done | bytes 2097184 | tf_op jit(solution)/shard_map/ppermute | solution.py:14
  361.5 0.0 collective-permute-start.6
  361.5 0.0 copy-start.2
  361.6 0.0 copy-start.4
  361.6 0.0 copy-start.8
  361.6 0.0 copy-start.10
  361.6 8.7 %broadcast_in_dim.3 = f32[4096,1024]{1,0:T(8,128)} broadcast(f32[]{:T(128)} %constant.56.clone.1), dimensions={} | broadcast | bytes 16777220 | tf_op jit(solution)/shard_map/broadcast_in_dim | solution.py:12
  370.3 1.6 constant_dynamic-update-slice_fusion.7
  371.9 0.0 copy-done.2
  371.9 1.4 constant_dynamic-update-slice_fusion.6
  373.3 0.0 copy-done.4
  373.4 1.5 constant_dynamic-update-slice_fusion.5
  374.8 0.0 copy-done.6
  374.8 1.5 constant_dynamic-update-slice_fusion.4
  376.3 0.0 copy-done.8
  376.3 1.5 constant_dynamic-update-slice_fusion.3
  377.8 0.0 copy-done.10
  377.8 1.5 constant_dynamic-update-slice_fusion.2
  379.3 3.2 constant_dynamic-update-slice_fusion.1
  382.5 24.6 %collective-permute-done.6 = f32[512,1024]{1,0:T(8,128)} collective-permute-done((f32[512,1024]{1,0:T(8,128)}, f32[512,1024]{1,0:T(8,128)}, u32[]{:S(2)}, u32[]{:S(2)}) %collective-permute-start.6) | collective-permute-done | bytes 2097184 | tf_op jit(solution)/shard_map/ppermute | solution.py:14
  407.1 3.2 constant_dynamic-update-slice_fusion
  410.2 56.3 %add_bitcast_fusion = f32[512,1024]{0,1:T(8,128)S(1)} fusion(f32[1024,512]{1,0:T(8,128)} %reduce-scatter.2.cloned.1.call-done, f32[4096,1024]{1,0:T(8,128)} %constant_dynamic-update-slice_fusion, f32[512,4096]{1,0:T(8,128)} %param.4), kind=kOutput, calls=%fused_computation | convolution fusion | flops 25770328064 | bytes 29360128 | tf_op jit(solution)/shard_map/dot_general | solution.py:21
  466.6 1.8 copy.4
  (3 shorter events, 0.0 us)
Async XLA Ops:
  6.5 57.7 %copy-start = (f32[512,1024]{1,0:T(8,128)S(1)}, f32[512,1024]{1,0:T(8,128)}, u32[]{:S(2)}) copy-start(f32[512,1024]{1,0:T(8,128)} %param.3) | copy-start | bytes 6291460
  6.5 403.7 %reduce-scatter.2.cloned.1.call-start = ((), (), s32[]{:S(2)}) async-start(), calls=%async_computation.1 | async-start | bytes 10485760 | tf_op jit(solution)/shard_map/reduce_scatter | solution.py:25
  64.2 51.7 %collective-permute-start = (f32[512,1024]{1,0:T(8,128)S(1)}, f32[512,1024]{1,0:T(8,128)S(1)}, u32[]{:S(2)}, u32[]{:S(2)}) collective-permute-start(f32[512,1024]{1,0:T(8,128)S(1)} %copy-done), channel_id=1, source_target_pairs={{0,4},{4,8},{8,12},{12,16},{16,20},{20,24},{24,28},{28,0},{1,5},{5... | collective-permute-start | bytes 6291464 | tf_op jit(solution)/shard_map/ppermute | solution.py:14
  115.9 1.3 copy-start.1
  117.2 49.5 %collective-permute-start.1 = (f32[512,1024]{1,0:T(8,128)S(1)}, f32[512,1024]{1,0:T(8,128)S(1)}, u32[]{:S(2)}, u32[]{:S(2)}) collective-permute-start(f32[512,1024]{1,0:T(8,128)S(1)} %collective-permute-done), channel_id=1, source_target_pairs={{0,4},{4,8},{8,12},{12,16},{16,20},{20,24},{24,28},{28,0},{1,5},{5... | collective-permute-start | bytes 6291464 | tf_op jit(solution)/shard_map/ppermute | solution.py:14
  166.7 1.3 copy-start.3
  168.0 48.6 %collective-permute-start.2 = (f32[512,1024]{1,0:T(8,128)S(1)}, f32[512,1024]{1,0:T(8,128)S(1)}, u32[]{:S(2)}, u32[]{:S(2)}) collective-permute-start(f32[512,1024]{1,0:T(8,128)S(1)} %collective-permute-done.1), channel_id=1, source_target_pairs={{0,4},{4,8},{8,12},{12,16},{16,20},{20,24},{24,28},{28,0},{1,5},{5... | collective-permute-start | bytes 6291464 | tf_op jit(solution)/shard_map/ppermute | solution.py:14
  216.6 1.4 copy-start.5
  218.0 47.8 %collective-permute-start.3 = (f32[512,1024]{1,0:T(8,128)S(1)}, f32[512,1024]{1,0:T(8,128)S(1)}, u32[]{:S(2)}, u32[]{:S(2)}) collective-permute-start(f32[512,1024]{1,0:T(8,128)S(1)} %collective-permute-done.2), channel_id=1, source_target_pairs={{0,4},{4,8},{8,12},{12,16},{16,20},{20,24},{24,28},{28,0},{1,5},{5... | collective-permute-start | bytes 6291464 | tf_op jit(solution)/shard_map/ppermute | solution.py:14
  265.8 1.3 copy-start.7
  267.1 46.9 %collective-permute-start.4 = (f32[512,1024]{1,0:T(8,128)S(1)}, f32[512,1024]{1,0:T(8,128)S(1)}, u32[]{:S(2)}, u32[]{:S(2)}) collective-permute-start(f32[512,1024]{1,0:T(8,128)S(1)} %collective-permute-done.3), channel_id=1, source_target_pairs={{0,4},{4,8},{8,12},{12,16},{16,20},{20,24},{24,28},{28,0},{1,5},{5... | collective-permute-start | bytes 6291464 | tf_op jit(solution)/shard_map/ppermute | solution.py:14
  314.1 1.3 copy-start.9
  315.4 46.2 %collective-permute-start.5 = (f32[512,1024]{1,0:T(8,128)S(1)}, f32[512,1024]{1,0:T(8,128)}, u32[]{:S(2)}, u32[]{:S(2)}) collective-permute-start(f32[512,1024]{1,0:T(8,128)S(1)} %collective-permute-done.4), channel_id=1, source_target_pairs={{0,4},{4,8},{8,12},{12,16},{16,20},{20,24},{24,28},{28,0},{1,5},{5... | collective-permute-start | bytes 6291464 | tf_op jit(solution)/shard_map/ppermute | solution.py:14
  361.5 45.5 %collective-permute-start.6 = (f32[512,1024]{1,0:T(8,128)}, f32[512,1024]{1,0:T(8,128)}, u32[]{:S(2)}, u32[]{:S(2)}) collective-permute-start(f32[512,1024]{1,0:T(8,128)} %collective-permute-done.5), channel_id=1, source_target_pairs={{0,4},{4,8},{8,12},{12,16},{16,20},{20,24},{24,28},{28,0},{1,5},{5... | collective-permute-start | bytes 6291464 | tf_op jit(solution)/shard_map/ppermute | solution.py:14
  361.5 10.4 %copy-start.2 = (f32[512,1024]{1,0:T(8,128)S(1)}, f32[512,1024]{1,0:T(8,128)}, u32[]{:S(2)}) copy-start(f32[512,1024]{1,0:T(8,128)} %copy-done.1) | copy-start | bytes 6291460
  361.6 11.8 %copy-start.4 = (f32[512,1024]{1,0:T(8,128)S(1)}, f32[512,1024]{1,0:T(8,128)}, u32[]{:S(2)}) copy-start(f32[512,1024]{1,0:T(8,128)} %copy-done.3) | copy-start | bytes 6291460
  361.6 13.3 %copy-start.6 = (f32[512,1024]{1,0:T(8,128)S(1)}, f32[512,1024]{1,0:T(8,128)}, u32[]{:S(2)}) copy-start(f32[512,1024]{1,0:T(8,128)} %copy-done.5) | copy-start | bytes 6291460
  361.6 14.7 %copy-start.8 = (f32[512,1024]{1,0:T(8,128)S(1)}, f32[512,1024]{1,0:T(8,128)}, u32[]{:S(2)}) copy-start(f32[512,1024]{1,0:T(8,128)} %copy-done.7) | copy-start | bytes 6291460
  361.6 16.3 %copy-start.10 = (f32[512,1024]{1,0:T(8,128)S(1)}, f32[512,1024]{1,0:T(8,128)}, u32[]{:S(2)}) copy-start(f32[512,1024]{1,0:T(8,128)} %copy-done.9) | copy-start | bytes 6291460
Sparse Core Ops, SparseCore 0:
  64.3 74.1 reduce-scatter.1
